TPU v7x, 128 devices: a whole 4x4x4 slice. The times are simulated.
128 devices in a mesh: grp: 4 (over z_hi, core), blk: 32 (over x, z_lo, y).
Axes of the slice: x: 4, y: 4, z: 4 (z_hi: 2, z_lo: 2; z = z_hi * 2 + z_lo), core: 2. Of those that a mesh axis runs over, the one named last changes fastest.
Arguments:
- integrals: bfloat16 [32768, 32768], P('blk', 'grp'), may hold values from -0.046875 to 0.046875
- block_mask: int32 [256, 256], P('blk', 'grp'), may hold values from 0 to 1, as said below
- amplitudes: bfloat16 [32768, 1024], P(('grp', 'blk')), may hold values from -6 to 6
- pair_batches: int32 [8], replicated, may hold values from 0 to 7, each once
Outputs:
- ladder: bfloat16 [1024, 32768], P('grp', 'blk')
Inputs may be any that keep to these rules, and one draw needn't show every extreme that they name: `block_mask`: 0 or 1; the share of kept tiles rises from about a quarter in the first tile row to about three quarters in the last. `pair_batches`: each batch number once.
All inputs are finite; a program needn't handle non-finite values.
Results may differ from a plain program's by a relative error of at most 0.001.
Values may be sent and summed in bfloat16 or wider, within the bound.
No kernel may reach another device: no remote copies, remote signals or barrier semaphores. Data moves between devices by JAX's collectives and lax.ppermute only.
A program may use at most 128 MiB of HBM per device.

v0:
```python
import jax
import jax.numpy as jnp
from jax import lax
from jax.sharding import PartitionSpec as P

BLOCK = 128
BATCH = 128
NB = 8


def on_device(integrals, block_mask, amplitudes, pair_batches):
    rows_in = amplitudes.shape[0]
    grouped = amplitudes.reshape(rows_in, NB, BATCH)
    selector = (pair_batches[:, None] == jnp.arange(NB, dtype=jnp.int32)[None, :]).astype(
        jnp.bfloat16
    )
    picked = jnp.einsum("rnb,mn->rmb", grouped, selector, preferred_element_type=jnp.float32)
    chosen = picked.astype(jnp.bfloat16).reshape(rows_in, NB * BATCH)
    out_rows = integrals.shape[0]
    fragment = lax.all_gather(chosen, "blk", axis=0, tiled=True)
    number = fragment.shape[0]
    mcols = block_mask.astype(jnp.bfloat16)
    tiled = (
        integrals.reshape(out_rows // BLOCK, BLOCK, number // BLOCK, BLOCK)
        * mcols[:, None, :, None]
    )
    masked = tiled.reshape(out_rows, number)
    partial_sum = lax.dot_general(
        fragment, masked, (((0,), (1,)), ((), ())), preferred_element_type=jnp.float32
    )
    owned = lax.psum_scatter(partial_sum, "grp", scatter_dimension=0, tiled=True)
    return owned.astype(jnp.bfloat16)


def solution(mesh):
    in_specs = (P("blk", "grp"), P("blk", "grp"), P(("grp", "blk"), None), P())
    out_specs = P("grp", "blk")
    return jax.shard_map(
        on_device, mesh=mesh, in_specs=in_specs, out_specs=out_specs, check_vma=False
    )
```

profile of v0, /device:TPU:1, one launch (start us, length us, event | category | flops | bytes accessed | tf_op | source)
XLA Modules:
  0.0 298.4 jit_solution(4227521799634697145)
XLA Ops:
  6.5 0.0 all-gather.2.cloned.1.call-start
  6.5 1.1 copy.5
  7.7 1.0 convolution_convert_fusion
  8.7 0.9 copy.13
  9.6 0.0 all-gather.2.cloned.1.call-update
  9.6 0.0 reduce-scatter.2.cloned.1.call-start
  9.7 0.7 convert_element_type.15
  10.3 192.8 %all-gather.2.cloned.1.call-done = bf16[8192,1024]{1,0:T(8,128)(2,1)} async-done(((bf16[256,1024]{1,0:T(8,128)(2,1)}), bf16[8192,1024]{1,0:T(8,128)(2,1)}) %all-gather.2.cloned.1.call-update) | async-done | bytes 16777232 | tf_op jit(solution)/shard_map/all_gather | solution.py:20
  203.2 6.5 %mul.11 = bf16[8,128,64,128]{3,2,1,0:T(8,128)(2,1)} broadcast(bf16[8,64]{1,0:T(8,128)(2,1)S(1)} %convert_element_type.15), dimensions={0,2} | broadcast | bytes 16778240 | tf_op jit(solution)/shard_map/mul | solution.py:24
  209.6 29.5 %fusion = f32[1024,1024]{1,0:T(8,128)} fusion(bf16[8192,1024]{1,0:T(8,128)(2,1)} %all-gather.2.cloned.1.call-done, bf16[1024,8192]{1,0:T(8,128)(2,1)} %param.4, bf16[128,8,64,128]{3,2,1,0:T(8,128)(2,1)} %bitcast.17), kind=kOutput, calls=%fused_computation.1 | convolution fusion | flops 17188257792 | bytes 54525952 | tf_op jit(solution)/shard_map/dot_general | solution.py:28
  239.1 0.0 reduce-scatter.2.cloned.1.call-update
  239.1 50.3 %reduce-scatter.2.cloned.1.call-done = f32[256,1024]{1,0:T(8,128)} async-done(((f32[1024,1024]{1,0:T(8,128)}), f32[256,1024]{1,0:T(8,128)}) %reduce-scatter.2.cloned.1.call-update) | async-done | bytes 1048592 | tf_op jit(solution)/shard_map/reduce_scatter | solution.py:31
  289.5 2.1 convert_element_type.16
Async XLA Ops:
  6.5 196.6 %all-gather.2.cloned.1.call-start = ((), (), s32[]{:S(2)}) async-start(), calls=%async_computation.1 | async-start | bytes 17301504 | tf_op jit(solution)/shard_map/all_gather | solution.py:20
  9.6 279.9 %reduce-scatter.2.cloned.1.call-start = ((), (), s32[]{:S(2)}) async-start(), calls=%async_computation.2 | async-start | bytes 5242880 | tf_op jit(solution)/shard_map/reduce_scatter | solution.py:31
Sparse Core Ops, SparseCore 0:
  9.7 193.3 all-gather.1
  239.3 50.1 reduce-scatter.1
where the time goes:
time: 299 us; the launch traced here: 298 us
  waiting for transfers between devices  243 us (81%)
  matrix products  30.5 us (10%)
  between operations  13.4 us (4%)
  local copies, waits for them, and re-layouts  8.49 us (3%)
    all_gather x1, waiting for transfers between devices, on_device(): fragment = lax.all_gather(chosen, 'blk', axis=0, tiled=True)  193 us
    reduce_scatter x1, waiting for transfers between devices, on_device(): lax.psum_scatter(partial_sum, 'grp', scatter_dimension=0, tiled=True)  50.3 us
    dot_general x1, matrix products, on_device(): lax.dot_general(fragment, masked, (((0,), (1,)), ((), ())), preferred_ele...  29.5 us
    mul x1, local copies, waits for them, and re-layouts, on_device(): integrals.reshape(out_rows // BLOCK, BLOCK, number // BLOCK, BLOCK)  6.47 us
  transfers between devices with their start and end apart: 2, of which 2 were waited for; matrix products, arithmetic and copies ran while one was open for 0% of the time, Pallas kernels for 0%

commit v1 on v0

--- a/solution.py
+++ b/solution.py
@@ -17,7 +17,9 @@
     picked = jnp.einsum("rnb,mn->rmb", grouped, selector, preferred_element_type=jnp.float32)
     chosen = picked.astype(jnp.bfloat16).reshape(rows_in, NB * BATCH)
     out_rows = integrals.shape[0]
-    fragment = lax.all_gather(chosen, "blk", axis=0, tiled=True)
+    fragment = jnp.concatenate(
+        lax.all_to_all(jnp.stack([chosen] * lax.axis_size("blk")), "blk", 0, 0), axis=0
+    )
     number = fragment.shape[0]
     mcols = block_mask.astype(jnp.bfloat16)
     tiled = (

time: 299 us -> 457 us (1.53)
  waiting for transfers between devices: 243 us -> 387 us
  starting transfers between devices: 0.04 us -> 9.51 us
  local copies, waits for them, and re-layouts: 8.49 us -> 13.7 us
    all_to_all x0 -> x1, waiting for transfers between devices: none -> 306 us  [on_device(): lax.all_to_all(jnp.stack([chosen] * lax.axis_size('blk')), 'blk', 0, 0)]
    all_gather x1 -> x0, waiting for transfers between devices: 193 us -> none  [on_device(): fragment = lax.all_gather(chosen, 'blk', axis=0, tiled=True)]
    reduce_scatter x1, waiting for transfers between devices: 50.3 us -> 80.7 us  [on_device(): lax.psum_scatter(partial_sum, 'grp', scatter_dimension=0, tiled=True)]
    all_to_all x0 -> x1, starting transfers between devices: none -> 9.47 us  [on_device(): lax.all_to_all(jnp.stack([chosen] * lax.axis_size('blk')), 'blk', 0, 0)]
    another operation x0 -> x1, local copies, waits for them, and re-layouts: none -> 5.97 us  [on_device(): jnp.stack([chosen] * lax.axis_size('blk'))]
where the time goes in v1:
time: 457 us; the launch traced here: 456 us
  waiting for transfers between devices  387 us (85%)
  matrix products  30.5 us (7%)
  local copies, waits for them, and re-layouts  13.7 us (3%)
  between operations  13.4 us (3%)
  starting transfers between devices  9.51 us (2%)
    all_to_all x1, waiting for transfers between devices, on_device(): lax.all_to_all(jnp.stack([chosen] * lax.axis_size('blk')), 'blk', 0, 0)  306 us
    reduce_scatter x1, waiting for transfers between devices, on_device(): lax.psum_scatter(partial_sum, 'grp', scatter_dimension=0, tiled=True)  80.7 us
    dot_general x1, matrix products, on_device(): lax.dot_general(fragment, masked, (((0,), (1,)), ((), ())), preferred_ele...  29.5 us
    all_to_all x1, starting transfers between devices, on_device(): lax.all_to_all(jnp.stack([chosen] * lax.axis_size('blk')), 'blk', 0, 0)  9.47 us
  transfers between devices with their start and end apart: 2, of which 2 were waited for; matrix products, arithmetic and copies ran while one was open for 0% of the time, Pallas kernels for 0%

profile of v1, /device:TPU:1, one launch (start us, length us, event | category | flops | bytes accessed | tf_op | source)
XLA Modules:
  0.0 456.2 jit_solution(16161924259358618020)
XLA Ops:
  6.5 1.1 copy.5
  7.7 1.0 convolution_convert_fusion
  8.7 0.1 copy.13
  8.8 6.0 %stack.3 = bf16[32,256,1024]{2,1,0:T(8,128)(2,1)} broadcast(bf16[256,1024]{1,0:T(8,128)(2,1)S(1)} %bitcast.19), dimensions={1,2} | broadcast | bytes 17301504 | tf_op jit(solution)/shard_map/stack | solution.py:21
  14.8 0.0 copy-start
  14.8 9.5 %all-to-all-start = ((bf16[32,256,1024]{2,1,0:T(8,128)(2,1)}), bf16[32,256,1024]{2,1,0:T(8,128)(2,1)}, u32[]{:S(2)}, u32[]{:S(2)}) async-start(bf16[32,256,1024]{2,1,0:T(8,128)(2,1)} %stack.3), calls=%async_computation | async-start | bytes 33554432 | tf_op jit(solution)/shard_map/all_to_all | solution.py:21
  24.2 0.0 reduce-scatter.2.cloned.1.call-start
  24.3 0.0 copy-done
  24.3 306.3 %all-to-all-done = bf16[32,256,1024]{2,1,0:T(8,128)(2,1)} async-done(((bf16[32,256,1024]{2,1,0:T(8,128)(2,1)}), bf16[32,256,1024]{2,1,0:T(8,128)(2,1)}, u32[]{:S(2)}, u32[]{:S(2)}) %all-to-all-start) | async-done | bytes 16777248 | tf_op jit(solution)/shard_map/all_to_all | solution.py:21
  330.6 6.5 %mul.11 = bf16[8,128,64,128]{3,2,1,0:T(8,128)(2,1)} broadcast(bf16[8,64]{1,0:T(8,128)(2,1)S(1)} %convert_element_type.15), dimensions={0,2} | broadcast | bytes 16778240 | tf_op jit(solution)/shard_map/mul | solution.py:26
  337.1 29.5 %fusion = f32[1024,1024]{1,0:T(8,128)} fusion(bf16[8192,1024]{1,0:T(8,128)(2,1)} %bitcast.2, bf16[1024,8192]{1,0:T(8,128)(2,1)} %param.4, bf16[128,8,64,128]{3,2,1,0:T(8,128)(2,1)} %bitcast.18), kind=kOutput, calls=%fused_computation.1 | convolution fusion | flops 17188257792 | bytes 54525952 | tf_op jit(solution)/shard_map/dot_general | solution.py:30
  366.5 0.0 reduce-scatter.2.cloned.1.call-update
  366.6 80.7 %reduce-scatter.2.cloned.1.call-done = f32[256,1024]{1,0:T(8,128)} async-done(((f32[1024,1024]{1,0:T(8,128)}), f32[256,1024]{1,0:T(8,128)}) %reduce-scatter.2.cloned.1.call-update) | async-done | bytes 1048592 | tf_op jit(solution)/shard_map/reduce_scatter | solution.py:33
  447.3 2.1 convert_element_type.16
  (1 shorter events, 0.0 us)
Async XLA Ops:
  14.8 9.5 %copy-start = (s32[8,64]{1,0:T(8,128)S(1)}, s32[8,64]{1,0:T(8,128)}, u32[]{:S(2)}) copy-start(s32[8,64]{1,0:T(8,128)} %param.5) | copy-start | bytes 6148
  14.8 315.8 %all-to-all-start = ((bf16[32,256,1024]{2,1,0:T(8,128)(2,1)}), bf16[32,256,1024]{2,1,0:T(8,128)(2,1)}, u32[]{:S(2)}, u32[]{:S(2)}) async-start(bf16[32,256,1024]{2,1,0:T(8,128)(2,1)} %stack.3), calls=%async_computation | async-start | bytes 33554432 | tf_op jit(solution)/shard_map/all_to_all | solution.py:21
  24.2 423.1 %reduce-scatter.2.cloned.1.call-start = ((), (), s32[]{:S(2)}) async-start(), calls=%async_computation.2 | async-start | bytes 5242880 | tf_op jit(solution)/shard_map/reduce_scatter | solution.py:33
Sparse Core Ops, SparseCore 0:
  366.7 80.5 reduce-scatter.1
